TPU v7x, 32 devices: a whole 2x2x4 slice. The times are simulated.
32 devices in a mesh: gz: 16 (over z, y, core), ta: 2 (over x).
Axes of the slice: x: 2, y: 2, z: 4, core: 2. Of those that a mesh axis runs over, the one named last changes fastest.
Arguments:
- outputs_fwd: bfloat16 [4, 32, 64, 1280], P('ta', 'gz'), may hold values from -6 to 6
- cotangent: bfloat16 [4, 32, 64, 1280], P('ta', 'gz'), may hold values from -6 to 6
- spatial_weight: bfloat16 [3, 64, 288], replicated, may hold values from -0.21875 to 0.21875
- hidden_bias: float32 [64], replicated, may hold values from -1 to 1
- temporal_weight: bfloat16 [3, 32, 64], replicated, may hold values from -0.4375 to 0.4375
Outputs:
- rebuilt: bfloat16 [4, 32, 32, 1280], P('ta', 'gz')
- grad_in: bfloat16 [4, 32, 32, 1280], P('ta', 'gz')
- grad_spatial: float32 [3, 64, 288], replicated
- grad_bias: float32 [64], replicated
- grad_temporal: float32 [3, 32, 64], replicated
All inputs are finite; a program needn't handle non-finite values.
Results may differ from a plain program's by a relative error of at most 0.0075.
Values may be sent and summed in bfloat16 or wider, within the bound.
A program may use at most 64 MiB of HBM per device.

v0:
```python
import math

import jax
import jax.numpy as jnp
from jax import lax
from jax.sharding import PartitionSpec as P

ROWS = 8
COLS = 160


def with_halo(cells, sides, width, closed):
    for axis, dim in sides:
        count = lax.axis_size(axis)
        ends = count if closed else count - 1
        head = lax.slice_in_dim(cells, 0, width, axis=dim)
        tail = lax.slice_in_dim(cells, cells.shape[dim] - width, cells.shape[dim], axis=dim)
        cells = jnp.concatenate(
            [
                lax.ppermute(tail, axis, [(i, (i + 1) % count) for i in range(ends)]),
                cells,
                lax.ppermute(head, axis, [((i + 1) % count, i) for i in range(ends)]),
            ],
            axis=dim,
        )
    return cells


def unfold(field):
    leading = field.shape[:-1]
    planar = field.reshape(leading + (ROWS, COLS))
    padded = jnp.pad(planar, [(0, 0)] * len(leading) + [(1, 1), (1, 1)])
    windows = [
        padded[..., row_off : row_off + ROWS, col_off : col_off + COLS]
        for row_off in range(3)
        for col_off in range(3)
    ]
    stacked = jnp.stack(windows, axis=-4)
    return stacked.reshape(leading[:-1] + (9 * leading[-1], ROWS * COLS))


def spatial(columns, spatial_weight, plane_count):
    total = jnp.einsum(
        "oi,fzir->fzor",
        spatial_weight[0],
        columns[:, 0:plane_count],
        preferred_element_type=jnp.float32,
    )
    total = total + jnp.einsum(
        "oi,fzir->fzor",
        spatial_weight[1],
        columns[:, 1 : plane_count + 1],
        preferred_element_type=jnp.float32,
    )
    total = total + jnp.einsum(
        "oi,fzir->fzor",
        spatial_weight[2],
        columns[:, 2 : plane_count + 2],
        preferred_element_type=jnp.float32,
    )
    return total


def temporal_back(temporal_weight, grad_around, frame_count):
    through = jnp.einsum(
        "oi,fzor->fzir",
        temporal_weight[0],
        grad_around[2 : frame_count + 2],
        preferred_element_type=jnp.float32,
    )
    through = through + jnp.einsum(
        "oi,fzor->fzir",
        temporal_weight[1],
        grad_around[1 : frame_count + 1],
        preferred_element_type=jnp.float32,
    )
    through = through + jnp.einsum(
        "oi,fzor->fzir",
        temporal_weight[2],
        grad_around[0:frame_count],
        preferred_element_type=jnp.float32,
    )
    return through


def hidden_gradient(through, hidden_in):
    sigmoid_val = jax.nn.sigmoid(hidden_in)
    return (through * sigmoid_val * (1.0 + hidden_in * (1.0 - sigmoid_val))).astype(jnp.bfloat16)


def shards(outputs_fwd, cotangent, spatial_weight, hidden_bias, temporal_weight):
    half = spatial_weight.shape[2] // 9
    hidden_count = spatial_weight.shape[1]
    front_half = outputs_fwd[:, :, :half]
    back_half = outputs_fwd[:, :, half:]
    grad_front = cotangent[:, :, :half]
    grad_back = cotangent[:, :, half:]
    frame_count = front_half.shape[0]
    plane_count = front_half.shape[1]
    bias_row = hidden_bias[None, None, :, None]
    depth_rim = 1
    padded_wide = with_halo(front_half, (("gz", 1),), depth_rim, False)
    columns = unfold(padded_wide)
    hidden_in = spatial(columns, spatial_weight, plane_count) + bias_row
    active = jax.nn.silu(hidden_in).astype(jnp.bfloat16)
    beside_all = with_halo(active, (("ta", 0),), 1, True)
    mapped = jnp.einsum(
        "oi,fzir->fzor",
        temporal_weight[0],
        beside_all[0:frame_count],
        preferred_element_type=jnp.float32,
    )
    mapped = mapped + jnp.einsum(
        "oi,fzir->fzor",
        temporal_weight[1],
        beside_all[1 : frame_count + 1],
        preferred_element_type=jnp.float32,
    )
    mapped = mapped + jnp.einsum(
        "oi,fzir->fzor",
        temporal_weight[2],
        beside_all[2 : frame_count + 2],
        preferred_element_type=jnp.float32,
    )
    rebuilt = (back_half.astype(jnp.float32) - mapped).astype(jnp.bfloat16)
    grad_around = with_halo(grad_back, (("ta", 0),), 1, True)
    through = temporal_back(temporal_weight, grad_around, frame_count)
    temporal_grad = jnp.stack(
        [
            jnp.einsum(
                "fzor,fzir->oi",
                grad_back,
                beside_all[offset : offset + frame_count],
                preferred_element_type=jnp.float32,
            )
            for offset in range(3)
        ]
    )
    hidden_grad = hidden_gradient(through, hidden_in)
    spatial_grad = jnp.stack(
        [
            jnp.einsum(
                "fzor,fzir->oi",
                hidden_grad,
                columns[:, depth : depth + plane_count],
                preferred_element_type=jnp.float32,
            )
            for depth in range(3)
        ]
    )
    bias_grad = jnp.einsum("fzor->o", hidden_grad.astype(jnp.float32))
    grad_planes = with_halo(hidden_grad, (("gz", 1),), 1, False)
    flipped = (
        spatial_weight.reshape((3, hidden_count, 9, half))[:, :, ::-1]
        .transpose((0, 3, 2, 1))
        .reshape((3, half, 9 * hidden_count))
    )

    def adjoint_frame(frame_planes):
        grad_columns = unfold(frame_planes)
        total = jnp.einsum(
            "ci,zir->zcr",
            flipped[0],
            grad_columns[2 : plane_count + 2],
            preferred_element_type=jnp.float32,
        )
        total = total + jnp.einsum(
            "ci,zir->zcr",
            flipped[1],
            grad_columns[1 : plane_count + 1],
            preferred_element_type=jnp.float32,
        )
        total = total + jnp.einsum(
            "ci,zir->zcr",
            flipped[2],
            grad_columns[0:plane_count],
            preferred_element_type=jnp.float32,
        )
        return total

    input_grad = lax.map(adjoint_frame, grad_planes)
    grad_in = (grad_front.astype(jnp.float32) + input_grad).astype(jnp.bfloat16)
    totals = lax.psum((spatial_grad, bias_grad, temporal_grad), ("gz", "ta"))
    factor = 1.0 / math.sqrt(
        frame_count * lax.axis_size("ta") * plane_count * lax.axis_size("gz") * ROWS * COLS
    )
    return (rebuilt, grad_in, totals[0] * factor, totals[1] * factor, totals[2] * factor)


def solution(mesh):
    placed = (P("ta", "gz", None, None), P("ta", "gz", None, None), P(), P(), P())
    return jax.shard_map(
        shards,
        mesh=mesh,
        in_specs=placed,
        out_specs=(P("ta", "gz", None, None), P("ta", "gz", None, None), P(), P(), P()),
        check_vma=False,
    )
```

profile of v0, /device:TPU:0, one launch (start us, length us, event | category | flops | bytes accessed | tf_op | source)
XLA Modules:
  0.0 338.4 jit_solution(7033846811327867473)
XLA Ops:
  7.2 1.1 fusion.125
  8.3 2.4 collective-permute-start
  10.8 1.3 collective-permute-start.1
  12.1 1.7 fusion.123
  13.7 2.3 collective-permute-start.4
  16.1 1.7 slice.236
  17.8 1.1 copy.41
  19.3 1.4 fusion.99
  20.8 1.3 reshape.45
  22.1 1.3 stack.118
  23.5 1.5 fusion.56
  25.0 1.2 fusion.58
  26.2 1.6 fusion.60
  27.8 1.4 fusion.62
  29.3 1.0 bitcast_dynamic-update-slice_fusion
  30.3 1.4 fusion.64
  31.7 1.7 fusion.66
  33.4 1.2 fusion.68
  34.6 1.6 fusion.70
  36.2 15.8 %reshape.46 = bf16[2,4,288,1280]{3,2,1,0:T(8,128)(2,1)} reshape(bf16[2,4,9,32,8,160]{5,4,3,2,1,0:T(8,128)(2,1)} %fusion.70) | data formatting | bytes 11796480 | tf_op jit(solution)/shard_map/reshape | solution.py:39
  52.0 2.7 fusion.40
  54.7 2.6 convolution_add_fusion.4
  57.4 0.9 multiply_convert_fusion
  58.4 1.5 fusion.87
  59.9 1.8 convert_reduce_fusion
  61.7 1.1 fusion.49
  62.8 1.1 fusion.46
  63.9 1.1 fusion.52
  65.1 1.1 fusion.101
  66.1 0.9 fusion.124
  67.0 0.7 pad_maximum_fusion.2
  67.8 4.3 %collective-permute-start.6 = (bf16[2,1,64,1280]{3,2,1,0:T(8,128)(2,1)S(1)}, bf16[2,1,64,1280]{3,2,1,0:T(8,128)(2,1)S(1)}, u32[]{:S(2)}, u32[]{:S(2)}) collective-permute-start(bf16[2,1,64,1280]{3,2,1,0:T(8,128)(2,1)S(1)} %get-tuple-element.72), channel_id=1, source_target_pairs={{0,2},{2,4},{4,6},{6,8},{8,10},{10,12},{12,14},{14,16},{16,18},{18... | collective-permute-start | bytes 983048 | tf_op jit(solution)/shard_map/ppermute | solution.py:20
  72.1 1.3 collective-permute-start.7
  73.4 1.6 collective-permute-start.2
  75.8 124.2 %all-reduce.5.cloned.1.call-done = f32[3,64,288]{2,1,0:T(8,128)} async-done(((f32[3,64,288]{2,1,0:T(8,128)}), f32[3,64,288]{2,1,0:T(8,128)}) %all-reduce.5.cloned.1.call-update) | async-done | bytes 221200 | tf_op jit(solution)/shard_map/psum | solution.py:183
  200.0 1.7 broadcast_multiply_fusion
  201.7 1.2 pad_maximum_fusion
  202.9 77.5 %while.12 = (s32[]{:T(128)}, f32[2,2,32,1280]{3,2,1,0:T(8,128)}, bf16[2,4,64,1280]{3,2,1,0:T(8,128)(2,1)}, bf16[3,32,576]{2,1,0:T(8,128)(2,1)S(1)}, s32[]{:T(128)}) while((s32[]{:T(128)}, f32[2,2,32,1280]{3,2,1,0:T(8,128)}, bf16[2,4,64,1280]{3,2,1,0:T(8,128)(2,1)}, bf16[3,32,576]{2,1,0:T(8,128)(2,1)S(1)}, s32[]{:T(128)}) %tuple.40), condition=%wide.region_1.2_spmd, body=%wide.region_0.1_spmd.sunk | while | flops 283279360 | bytes 69722216 | solution.py:181
  202.9 1.1 constant_dynamic-slice_fusion.2
  204.1 1.3 reshape.65
  205.4 1.3 stack.133
  209.1 0.8 fusion.162
  210.7 5.4 %fusion.165 = (bf16[2,9,64,8,160]{4,3,2,1,0:T(8,128)(2,1)}, bf16[2,9,64,8,160]{4,3,2,1,0:T(8,128)(2,1)}, bf16[2,9,64,8,160]{4,3,2,1,0:T(8,128)(2,1)}) fusion(bf16[4,9,64,8,160]{4,3,2,1,0:T(8,128)(2,1)S(1)} %fusion.164), kind=kLoop, calls=%fused_computation.155.clone.1 | loop fusion | bytes 17694720 | tf_op jit(solution)/shard_map/while/body/eval_jaxpr/slice | solution.py:176
  216.1 7.4 %slice.457 = bf16[2,576,1280]{2,1,0:T(8,128)(2,1)S(1)} reshape(bf16[2,9,64,8,160]{4,3,2,1,0:T(8,128)(2,1)} %get-tuple-element.112) | data formatting | bytes 5898240 | tf_op jit(solution)/shard_map/while/body/eval_jaxpr/slice | solution.py:164
  224.1 7.4 %slice.458 = bf16[2,576,1280]{2,1,0:T(8,128)(2,1)S(1)} reshape(bf16[2,9,64,8,160]{4,3,2,1,0:T(8,128)(2,1)} %get-tuple-element.113) | data formatting | bytes 5898240 | tf_op jit(solution)/shard_map/while/body/eval_jaxpr/slice | solution.py:170
  231.5 1.3 convolution_add_fusion.7
  232.9 7.4 %slice.459 = bf16[2,576,1280]{2,1,0:T(8,128)(2,1)S(1)} reshape(bf16[2,9,64,8,160]{4,3,2,1,0:T(8,128)(2,1)} %get-tuple-element.114) | data formatting | bytes 5898240 | tf_op jit(solution)/shard_map/while/body/eval_jaxpr/slice | solution.py:176
  240.4 1.4 fusion.167
  241.7 1.1 constant_dynamic-slice_fusion.2
  242.8 1.3 reshape.65
  244.2 1.3 stack.133
  247.8 0.8 fusion.162
  249.5 5.4 %fusion.165 = (bf16[2,9,64,8,160]{4,3,2,1,0:T(8,128)(2,1)}, bf16[2,9,64,8,160]{4,3,2,1,0:T(8,128)(2,1)}, bf16[2,9,64,8,160]{4,3,2,1,0:T(8,128)(2,1)}) fusion(bf16[4,9,64,8,160]{4,3,2,1,0:T(8,128)(2,1)S(1)} %fusion.164), kind=kLoop, calls=%fused_computation.155.clone.1 | loop fusion | bytes 17694720 | tf_op jit(solution)/shard_map/while/body/eval_jaxpr/slice | solution.py:176
  254.9 7.4 %slice.457 = bf16[2,576,1280]{2,1,0:T(8,128)(2,1)S(1)} reshape(bf16[2,9,64,8,160]{4,3,2,1,0:T(8,128)(2,1)} %get-tuple-element.112) | data formatting | bytes 5898240 | tf_op jit(solution)/shard_map/while/body/eval_jaxpr/slice | solution.py:164
  262.9 7.4 %slice.458 = bf16[2,576,1280]{2,1,0:T(8,128)(2,1)S(1)} reshape(bf16[2,9,64,8,160]{4,3,2,1,0:T(8,128)(2,1)} %get-tuple-element.113) | data formatting | bytes 5898240 | tf_op jit(solution)/shard_map/while/body/eval_jaxpr/slice | solution.py:170
  270.3 1.3 convolution_add_fusion.7
  271.7 7.4 %slice.459 = bf16[2,576,1280]{2,1,0:T(8,128)(2,1)S(1)} reshape(bf16[2,9,64,8,160]{4,3,2,1,0:T(8,128)(2,1)} %get-tuple-element.114) | data formatting | bytes 5898240 | tf_op jit(solution)/shard_map/while/body/eval_jaxpr/slice | solution.py:176
  279.1 1.3 fusion.167
  280.5 2.1 add_convert_fusion
  282.6 1.5 convolution_bitcast_fusion.1
  284.0 1.5 convolution_bitcast_fusion
  285.5 41.7 %all-reduce.2 = (f32[64]{0:T(128)S(1)}, f32[3,32,64]{2,1,0:T(8,128)S(1)}) all-reduce(f32[64]{0:T(128)S(1)} %get-tuple-element.82, f32[3,32,64]{2,1,0:T(8,128)S(1)} %pad_maximum_fusion.3), channel_id=1, replica_groups=mesh['gz'=16,'ta'=2] {'gz','ta'}, use_global_device_ids=true, to_apply=%region_4.5 | all-reduce | flops 6208 | bytes 49664 | tf_op jit(solution)/shard_map/psum | solution.py:183
  328.4 1.2 fusion.77
  329.6 1.9 fusion.45
  (70 shorter events, 10.2 us)
Async XLA Ops:
  7.2 13.6 %slice-start = ((bf16[2,2,64,1280]{3,2,1,0:T(8,128)(2,1)}), bf16[2,2,32,1280]{3,2,1,0:T(8,128)(2,1)S(1)}, s32[]{:S(2)}) async-start(bf16[2,2,64,1280]{3,2,1,0:T(8,128)(2,1)} %param.7), calls=%async_computation.1 | async-start | bytes 655360 | tf_op jit(solution)/shard_map/slice | solution.py:94
  7.2 12.1 %copy-start.4 = (bf16[2,2,64,1280]{3,2,1,0:T(8,128)(2,1)S(1)}, bf16[2,2,64,1280]{3,2,1,0:T(8,128)(2,1)}, u32[]{:S(2)}) copy-start(bf16[2,2,64,1280]{3,2,1,0:T(8,128)(2,1)} %param.8) | copy-start | bytes 1966084
  7.2 12.1 %copy-start.11 = (bf16[3,32,64]{2,1,0:T(8,128)(2,1)S(1)}, bf16[3,32,64]{2,1,0:T(8,128)(2,1)}, u32[]{:S(2)}) copy-start(bf16[3,32,64]{2,1,0:T(8,128)(2,1)} %param.11) | copy-start | bytes 36868
  7.2 192.8 %all-reduce.5.cloned.1.call-start = ((), (), s32[]{:S(2)}) async-start(), calls=%async_computation | async-start | bytes 589824 | tf_op jit(solution)/shard_map/psum | solution.py:183
  8.3 12.4 %collective-permute-start = (bf16[2,1,32,1280]{3,2,1,0:T(8,128)(2,1)S(1)}, bf16[2,1,32,1280]{3,2,1,0:T(8,128)(2,1)S(1)}, u32[]{:S(2)}, u32[]{:S(2)}) collective-permute-start(bf16[2,1,32,1280]{3,2,1,0:T(8,128)(2,1)S(1)} %get-tuple-element.78), channel_id=1, source_target_pairs={{0,2},{2,4},{4,6},{6,8},{8,10},{10,12},{12,14},{14,16},{16,18},{18... | collective-permute-start | bytes 491528 | tf_op jit(solution)/shard_map/ppermute | solution.py:20
  10.8 10.0 %collective-permute-start.1 = (bf16[2,1,32,1280]{3,2,1,0:T(8,128)(2,1)S(1)}, bf16[2,1,32,1280]{3,2,1,0:T(8,128)(2,1)S(1)}, u32[]{:S(2)}, u32[]{:S(2)}) collective-permute-start(bf16[2,1,32,1280]{3,2,1,0:T(8,128)(2,1)S(1)} %get-tuple-element.79), channel_id=1, source_target_pairs={{2,0},{4,2},{6,4},{8,6},{10,8},{12,10},{14,12},{16,14},{18,16},{20... | collective-permute-start | bytes 491528 | tf_op jit(solution)/shard_map/ppermute | solution.py:22
  13.7 46.1 %collective-permute-start.4 = (bf16[1,2,32,1280]{3,2,1,0:T(8,128)(2,1)}, bf16[1,2,32,1280]{3,2,1,0:T(8,128)(2,1)}, u32[]{:S(2)}, u32[]{:S(2)}) collective-permute-start(bf16[1,2,32,1280]{3,2,1,0:T(8,128)(2,1)} %get-tuple-element.74), channel_id=1, source_target_pairs={{1,0},{0,1},{3,2},{2,3},{5,4},{4,5},{7,6},{6,7},{9,8},{8,9},{11,10... | collective-permute-start | bytes 491528 | tf_op jit(solution)/shard_map/ppermute | solution.py:22
  16.1 42.3 %collective-permute-start.5 = (bf16[1,2,32,1280]{3,2,1,0:T(8,128)(2,1)S(1)}, bf16[1,2,32,1280]{3,2,1,0:T(8,128)(2,1)}, u32[]{:S(2)}, u32[]{:S(2)}) collective-permute-start(bf16[1,2,32,1280]{3,2,1,0:T(8,128)(2,1)S(1)} %get-tuple-element.75), channel_id=1, source_target_pairs={{0,1},{1,0},{2,3},{3,2},{4,5},{5,4},{6,7},{7,6},{8,9},{9,8},{10,11... | collective-permute-start | bytes 491528 | tf_op jit(solution)/shard_map/ppermute | solution.py:20
  36.2 15.8 %copy-start.10 = (bf16[3,64,288]{2,1,0:T(8,128)(2,1)S(1)}, bf16[3,64,288]{2,1,0:T(8,128)(2,1)}, u32[]{:S(2)}) copy-start(bf16[3,64,288]{2,1,0:T(8,128)(2,1)} %param.9) | copy-start | bytes 331780
  52.0 5.4 %copy-start.1 = (bf16[2,4,288,1280]{3,2,1,0:T(8,128)(2,1)S(1)}, bf16[2,4,288,1280]{3,2,1,0:T(8,128)(2,1)}, u32[]{:S(2)}) copy-start(bf16[2,4,288,1280]{3,2,1,0:T(8,128)(2,1)} %reshape.46) | copy-start | bytes 17694724
  54.7 2.7 copy-start.12
  57.4 1.0 copy-start.8
  57.4 2.5 copy-start.9
  58.3 17.2 %copy-start.2 = (bf16[2,2,64,1280]{3,2,1,0:T(8,128)(2,1)}, bf16[2,2,64,1280]{3,2,1,0:T(8,128)(2,1)S(1)}, u32[]{:S(2)}) copy-start(bf16[2,2,64,1280]{3,2,1,0:T(8,128)(2,1)S(1)} %get-tuple-element.80) | copy-start | bytes 1966084
  65.0 10.5 %copy-start.5 = (bf16[2,2,64,1280]{3,2,1,0:T(8,128)(2,1)S(1)}, bf16[2,2,64,1280]{3,2,1,0:T(8,128)(2,1)}, u32[]{:S(2)}) copy-start(bf16[2,2,64,1280]{3,2,1,0:T(8,128)(2,1)} %param.8) | copy-start | bytes 1966084
  67.8 133.9 %collective-permute-start.6 = (bf16[2,1,64,1280]{3,2,1,0:T(8,128)(2,1)S(1)}, bf16[2,1,64,1280]{3,2,1,0:T(8,128)(2,1)S(1)}, u32[]{:S(2)}, u32[]{:S(2)}) collective-permute-start(bf16[2,1,64,1280]{3,2,1,0:T(8,128)(2,1)S(1)} %get-tuple-element.72), channel_id=1, source_target_pairs={{0,2},{2,4},{4,6},{6,8},{8,10},{10,12},{12,14},{14,16},{16,18},{18... | collective-permute-start | bytes 983048 | tf_op jit(solution)/shard_map/ppermute | solution.py:20
  72.1 129.6 %collective-permute-start.7 = (bf16[2,1,64,1280]{3,2,1,0:T(8,128)(2,1)S(1)}, bf16[2,1,64,1280]{3,2,1,0:T(8,128)(2,1)S(1)}, u32[]{:S(2)}, u32[]{:S(2)}) collective-permute-start(bf16[2,1,64,1280]{3,2,1,0:T(8,128)(2,1)S(1)} %get-tuple-element.73), channel_id=1, source_target_pairs={{2,0},{4,2},{6,4},{8,6},{10,8},{12,10},{14,12},{16,14},{18,16},{20... | collective-permute-start | bytes 983048 | tf_op jit(solution)/shard_map/ppermute | solution.py:22
  73.4 209.2 %collective-permute-start.2 = (bf16[1,2,64,1280]{3,2,1,0:T(8,128)(2,1)}, bf16[1,2,64,1280]{3,2,1,0:T(8,128)(2,1)}, u32[]{:S(2)}, u32[]{:S(2)}) collective-permute-start(bf16[1,2,64,1280]{3,2,1,0:T(8,128)(2,1)} %get-tuple-element.76), channel_id=1, source_target_pairs={{0,1},{1,0},{2,3},{3,2},{4,5},{5,4},{6,7},{7,6},{8,9},{9,8},{10,11... | collective-permute-start | bytes 983048 | tf_op jit(solution)/shard_map/ppermute | solution.py:20
  75.0 209.1 %collective-permute-start.3 = (bf16[1,2,64,1280]{3,2,1,0:T(8,128)(2,1)}, bf16[1,2,64,1280]{3,2,1,0:T(8,128)(2,1)}, u32[]{:S(2)}, u32[]{:S(2)}) collective-permute-start(bf16[1,2,64,1280]{3,2,1,0:T(8,128)(2,1)} %get-tuple-element.77), channel_id=1, source_target_pairs={{1,0},{0,1},{3,2},{2,3},{5,4},{4,5},{7,6},{6,7},{9,8},{8,9},{11,10... | collective-permute-start | bytes 983048 | tf_op jit(solution)/shard_map/ppermute | solution.py:22
  232.9 7.5 %copy-start = (f32[2,1280,32]{1,2,0:T(8,128)S(1)}, f32[2,1280,32]{1,2,0:T(8,128)}, u32[]{:S(2)}) copy-start(f32[2,1280,32]{1,2,0:T(8,128)} %convolution_add_fusion.7) | copy-start | bytes 983044 | tf_op jit(solution)/shard_map/while
  271.6 7.5 %copy-start = (f32[2,1280,32]{1,2,0:T(8,128)S(1)}, f32[2,1280,32]{1,2,0:T(8,128)}, u32[]{:S(2)}) copy-start(f32[2,1280,32]{1,2,0:T(8,128)} %convolution_add_fusion.7) | copy-start | bytes 983044 | tf_op jit(solution)/shard_map/while
  280.5 47.9 %copy-start.3 = (bf16[2,2,64,1280]{3,2,1,0:T(8,128)(2,1)S(1)}, bf16[2,2,64,1280]{3,2,1,0:T(8,128)(2,1)}, u32[]{:S(2)}) copy-start(bf16[2,2,64,1280]{3,2,1,0:T(8,128)(2,1)} %copy-done.2) | copy-start | bytes 1966084
  280.5 49.1 %copy-start.6 = (f32[2,2,1280,32]{2,3,1,0:T(8,128)S(1)}, f32[2,2,1280,32]{2,3,1,0:T(8,128)}, u32[]{:S(2)}) copy-start(f32[2,2,1280,32]{2,3,1,0:T(8,128)} %fusion.101) | copy-start | bytes 1966084
  280.5 49.1 %copy-start.7 = (bf16[2,2,64,1280]{3,2,1,0:T(8,128)(2,1)S(1)}, bf16[2,2,64,1280]{3,2,1,0:T(8,128)(2,1)}, u32[]{:S(2)}) copy-start(bf16[2,2,64,1280]{3,2,1,0:T(8,128)(2,1)} %param.7) | copy-start | bytes 1966084
Sparse Core Ops, SparseCore 0:
  67.9 132.0 all-reduce.4
where the time goes:
time: 340 us; the launch traced here: 338 us
  waiting for transfers between devices  124 us (36%)
  local copies, waits for them, and re-layouts  109 us (32%)
  blocking collectives  41.7 us (12%)
  matrix products  28.3 us (8%)
  between operations  14.4 us (4%)
  starting transfers between devices  13.8 us (4%)
  other arithmetic  6.97 us (2%)
    psum x1, waiting for transfers between devices, shards(): totals = lax.psum((spatial_grad, bias_grad, temporal_grad), ('gz', 'ta'))  124 us
    psum x1, blocking collectives, shards(): totals = lax.psum((spatial_grad, bias_grad, temporal_grad), ('gz', 'ta'))  41.7 us
    slice x4, local copies, waits for them, and re-layouts, adjoint_frame(): grad_columns[0:plane_count]  25.7 us
    reshape x1, local copies, waits for them, and re-layouts, unfold(): return stacked.reshape(leading[:-1] + (9 * leading[-1], ROWS * COLS))  15.8 us
    slice x2, local copies, waits for them, and re-layouts, adjoint_frame(): grad_columns[1:plane_count + 1]  14.8 us
    slice x2, local copies, waits for them, and re-layouts, adjoint_frame(): grad_columns[2:plane_count + 2]  14.8 us
    unnamed x33, local copies, waits for them, and re-layouts  12.3 us
    ppermute x4, starting transfers between devices, with_halo(): lax.ppermute(tail, axis, [(i, (i + 1) % count) for i in range(ends)])  8.3 us
  transfers between devices with their start and end apart: 9, of which 1 were waited for; matrix products, arithmetic and copies ran while one was open for 38% of the time, Pallas kernels for 0%

commit v1 on v0

v1 whole, which is shorter than its diff:
```python
import functools
import math

import jax
import jax.numpy as jnp
from jax import lax
from jax.experimental import pallas as pl
from jax.experimental.pallas import tpu as pltpu
from jax.sharding import PartitionSpec as P

ROWS = 8
COLS = 160
F32 = jnp.float32
BF16 = jnp.bfloat16


def levels_of(gz_count, ta_count):
    bits = lambda count: [1 << i for i in range(count.bit_length() - 1)]
    gz_bits = [("gz", bit) for bit in bits(gz_count)]
    ta_bits = [("ta", bit) for bit in bits(ta_count)]
    return gz_bits[:1] + ta_bits + gz_bits[1:]


def nn(lhs, rhs):
    return lax.dot_general(lhs, rhs, (((1,), (0,)), ((), ())), preferred_element_type=F32)


def nt(lhs, rhs):
    return lax.dot_general(lhs, rhs, (((1,), (1,)), ((), ())), preferred_element_type=F32)


def tn(lhs, rhs):
    return lax.dot_general(lhs, rhs, (((0,), (0,)), ((), ())), preferred_element_type=F32)


def kernel(
    gz_count, ta_count, factor,
    x_ref, g_ref, wcat_ref, flip_ref, bias_ref, tw_ref,
    rebuilt_ref, gin_ref, gs_ref, gb_ref, gt_ref,
    cols, hcols, g3, yh, slope, act, hgr, parts, mown, msend, mrecv, psend, precv,
    acc, rs0s, rs0r, acc1, rs1s, rs1r, exs, exr, fin,
    ysem_s, ysem_r, gsem_s, gsem_r, msem_s, msem_r, psem_s, psem_r, asem_s, asem_r,
):
    frames, planes = x_ref.shape[0], x_ref.shape[1]
    half = x_ref.shape[2] // 2
    pix = x_ref.shape[3]
    hid = bias_ref.shape[0]
    me_g = lax.axis_index("gz")
    me_t = lax.axis_index("ta")
    has_l = me_g > 0
    has_r = me_g < gz_count - 1
    mesh_id = pl.DeviceIdType.MESH
    ta_r = lax.rem(me_t + 1, ta_count)
    ta_l = lax.rem(me_t + ta_count - 1, ta_count)
    levels = levels_of(gz_count, ta_count)

    def partner(level):
        axis, bit = levels[level]
        at = me_g if axis == "gz" else me_t
        has = lax.rem(at // bit, 2)
        other = at + bit - 2 * bit * has
        dev = (other, me_t) if axis == "gz" else (me_g, other)
        return dev, has

    barrier = pltpu.get_barrier_semaphore()

    def greet(dev):
        pl.semaphore_signal(barrier, inc=1, device_id=dev, device_id_type=mesh_id)

    greet((me_g, ta_r))
    greet((me_g, ta_l))
    for level in range(len(levels)):
        greet(partner(level)[0])

    @pl.when(has_l)
    def _():
        greet((me_g - 1, me_t))

    @pl.when(has_r)
    def _():
        greet((me_g + 1, me_t))

    beside = has_l.astype(jnp.int32) + has_r.astype(jnp.int32)
    pl.semaphore_wait(barrier, 2 + len(levels) + beside)

    def remote(src, dst, ssem, rsem, dev):
        return pltpu.make_async_remote_copy(
            src_ref=src, dst_ref=dst, send_sem=ssem, recv_sem=rsem, device_id=dev, device_id_type=mesh_id
        )

    y_right = remote(x_ref.at[:, planes - 1, 0:half], yh.at[0], ysem_s.at[0], ysem_r.at[0], (me_g + 1, me_t))
    y_left = remote(x_ref.at[:, 0, 0:half], yh.at[1], ysem_s.at[1], ysem_r.at[1], (me_g - 1, me_t))
    g_left = remote(
        g_ref.at[0, :, half : 2 * half], g3.at[frames - 1, :, 0:half], gsem_s.at[0], gsem_r.at[0], (me_g, ta_l)
    )
    g_right = remote(
        g_ref.at[frames - 1, :, half : 2 * half], g3.at[0, :, 2 * half : 3 * half], gsem_s.at[1], gsem_r.at[1], (me_g, ta_r)
    )
    pl.when(has_r)(y_right.start)
    pl.when(has_l)(y_left.start)
    g_left.start()
    g_right.start()

    for s in range(frames):
        for z in range(planes):
            for k in range(3):
                t = s + 1 - k
                if 0 <= t < frames:
                    g3[s, z, k * half : (k + 1) * half, :] = g_ref[t, z, half : 2 * half, :]

    place = lax.broadcasted_iota(jnp.int32, (1, pix), 1)
    column = lax.rem(place, COLS)
    col_ok = {-1: column > 0, 1: column < COLS - 1}
    row_ok = {-1: place >= COLS, 1: place < pix - COLS}

    def unfold(value, store):
        for c in (-1, 0, 1):
            moved = value
            if c != 0:
                moved = jnp.where(col_ok[c], pltpu.roll(value, (-c) % pix, 1), 0.0)
            for r in (-1, 0, 1):
                out = moved
                if r != 0:
                    out = jnp.where(row_ok[r], pltpu.roll(moved, (-r * COLS) % pix, 1), 0.0)
                store(3 * (r + 1) + c + 1, out.astype(BF16))

    window = 9 * half

    def unfold_y(value, t, plane):
        def store(w, out):
            base = plane * window + w * half
            cols[t, base : base + half, :] = out

        unfold(value.astype(F32), store)

    for t in range(frames):
        for z in range(planes):
            unfold_y(x_ref[t, z, 0:half, :], t, z + 1)

    @pl.when(has_l)
    def _():
        y_right.wait_recv()
        for t in range(frames):
            unfold_y(yh[0, t], t, 0)

    @pl.when(jnp.logical_not(has_l))
    def _():
        for t in range(frames):
            cols[t, 0:window, :] = jnp.zeros((window, pix), BF16)

    @pl.when(has_r)
    def _():
        y_left.wait_recv()
        for t in range(frames):
            unfold_y(yh[1, t], t, planes + 1)

    @pl.when(jnp.logical_not(has_r))
    def _():
        for t in range(frames):
            cols[t, (planes + 1) * window : (planes + 2) * window, :] = jnp.zeros((window, pix), BF16)

    wcat = wcat_ref[...]
    tw = tw_ref[...]
    bias = bias_ref[...]
    for t in range(frames):
        for z in range(planes):
            pre = nn(wcat, cols[t, z * window : (z + 3) * window, :]) + bias
            sig = jax.nn.sigmoid(pre)
            active = (pre * sig).astype(BF16)
            slope[t, z] = sig * (1.0 + pre * (1.0 - sig))
            act[t, z] = active
            mown[t, z] = nn(tw, active)
        if t == 0:
            for z in range(planes):
                msend[1, z] = mown[0, z, 2 * half : 3 * half, :].astype(BF16)
        if t == frames - 1:
            for z in range(planes):
                msend[0, z] = mown[t, z, 0:half, :].astype(BF16)
    m_right = remote(msend.at[0], mrecv.at[0], msem_s.at[0], msem_r.at[0], (me_g, ta_r))
    m_left = remote(msend.at[1], mrecv.at[1], msem_s.at[1], msem_r.at[1], (me_g, ta_l))
    m_right.start()
    m_left.start()

    g_left.wait_recv()
    g_right.wait_recv()
    ones = jnp.ones((8, pix), BF16)
    ssum = jnp.zeros((3 * window, hid), F32)
    tsum = jnp.zeros((3 * half, hid), F32)
    bsum = jnp.zeros((8, hid), F32)
    for t in range(frames):
        for z in range(planes):
            around = g3[t, z]
            hgrad = (tn(tw, around) * slope[t, z]).astype(BF16)
            hgr[t, z] = hgrad
            tsum = tsum + nt(around, act[t, z])
            bsum = bsum + nt(ones, hgrad)
            ssum = ssum + nt(cols[t, z * window : (z + 3) * window, :], hgrad)
    lines = acc.shape[0] // 2
    acc[0:lines, 0:hid] = ssum[0:window]
    acc[0:lines, hid : 2 * hid] = ssum[window : 2 * window]
    acc[lines : 2 * lines, 0:hid] = ssum[2 * window : 3 * window]
    acc[lines : lines + 3 * half, hid : 2 * hid] = tsum
    acc[lines + 3 * half : lines + 3 * half + 8, hid : 2 * hid] = bsum
    acc[lines + 3 * half + 8 : 2 * lines, hid : 2 * hid] = jnp.zeros((lines - 3 * half - 8, hid), F32)

    dev0, bit0 = partner(0)
    dev1, bit1 = partner(1)
    short = lines // 2
    rs0 = remote(rs0s, rs0r, asem_s.at[0], asem_r.at[0], dev0)
    rs1 = remote(rs1s, rs1r, asem_s.at[1], asem_r.at[1], dev1)
    quarter = fin.at[pl.ds(pl.multiple_of(bit0 * lines + bit1 * short, 16), short)]
    side = fin.at[pl.ds(pl.multiple_of(bit0 * lines, 16), lines)]
    last = len(levels)
    ag1 = remote(quarter, quarter, asem_s.at[last], asem_r.at[last], dev1)
    ag0 = remote(side, side, asem_s.at[last + 1], asem_r.at[last + 1], dev0)

    def ex(level):
        return remote(
            exs.at[level - 2], exr.at[level - 2], asem_s.at[level], asem_r.at[level], partner(level)[0]
        )

    def step_first():
        rs0s[...] = acc[pl.ds(pl.multiple_of((1 - bit0) * lines, 16), lines), :].astype(BF16)
        rs0.start()

    def step_second():
        rs0.wait_recv()
        acc1[...] = acc[pl.ds(pl.multiple_of(bit0 * lines, 16), lines), :] + rs0r[...].astype(F32)
        rs1s[...] = acc1[pl.ds(pl.multiple_of((1 - bit1) * short, 16), short), :].astype(BF16)
        rs1.start()

    def hand_on(level, value):
        if level < last:
            exs[level - 2] = value.astype(BF16)
            ex(level).start()
        else:
            fin[pl.ds(pl.multiple_of(bit0 * lines + bit1 * short, 16), short), :] = value.astype(BF16)
            ag1.start()

    def step_third():
        rs1.wait_recv()
        hand_on(2, acc1[pl.ds(pl.multiple_of(bit1 * short, 16), short), :] + rs1r[...].astype(F32))

    def step_ex(level):
        ex(level).wait_recv()
        hand_on(level + 1, exs[level - 2].astype(F32) + exr[level - 2].astype(F32))

    def step_gather():
        ag1.wait_recv()
        ag0.start()

    steps = [step_first, step_second, step_third]
    steps += [functools.partial(step_ex, level) for level in range(2, last)]
    steps += [step_gather]

    steps.pop(0)()

    flip = flip_ref[...]

    def p_right(t):
        return remote(psend.at[0, t], precv.at[0, t], psem_s.at[0, t], psem_r.at[0, t], (me_g + 1, me_t))

    def p_left(t):
        return remote(psend.at[1, t], precv.at[1, t], psem_s.at[1, t], psem_r.at[1, t], (me_g - 1, me_t))

    for t in range(frames):
        for z in range(planes):
            at = t * planes + z

            def store(w, out):
                hcols[at, w * hid : (w + 1) * hid, :] = out

            unfold(hgr[t, z].astype(F32), store)
            parts[t, z] = nn(flip, hcols[at])
            if z == 0:
                psend[1, t] = parts[t, z, 0:half, :].astype(BF16)
                pl.when(has_l)(p_left(t).start)
            if z == planes - 1:
                psend[0, t] = parts[t, z, 2 * half : 3 * half, :].astype(BF16)
                pl.when(has_r)(p_right(t).start)
            if len(steps) > 1:
                steps.pop(0)()

    m_right.wait_recv()
    m_left.wait_recv()
    for t in range(frames):
        for z in range(planes):
            total = mown[t, z, half : 2 * half, :]
            total = total + (mown[t - 1, z, 0:half, :] if t > 0 else mrecv[0, z].astype(F32))
            total = total + (mown[t + 1, z, 2 * half : 3 * half, :] if t < frames - 1 else mrecv[1, z].astype(F32))
            rebuilt_ref[t, z] = (x_ref[t, z, half : 2 * half, :].astype(F32) - total).astype(BF16)
    if len(steps) > 1:
        steps.pop(0)()

    @pl.when(has_l)
    def _():
        for t in range(frames):
            p_right(t).wait_recv()

    @pl.when(jnp.logical_not(has_l))
    def _():
        precv[0] = jnp.zeros_like(precv[0])

    @pl.when(has_r)
    def _():
        for t in range(frames):
            p_left(t).wait_recv()

    @pl.when(jnp.logical_not(has_r))
    def _():
        precv[1] = jnp.zeros_like(precv[1])

    for t in range(frames):
        for z in range(planes):
            total = parts[t, z, half : 2 * half, :]
            total = total + (parts[t, z - 1, 2 * half : 3 * half, :] if z > 0 else precv[0, t].astype(F32))
            total = total + (parts[t, z + 1, 0:half, :] if z < planes - 1 else precv[1, t].astype(F32))
            gin_ref[t, z] = (g_ref[t, z, 0:half, :].astype(F32) + total).astype(BF16)

    while steps:
        steps.pop(0)()
    ag0.wait_recv()
    top = fin[0:lines, :].astype(F32) * factor
    turned = top.T
    gs_ref[0] = turned[0:hid]
    gs_ref[1] = turned[hid : 2 * hid]
    low = fin[lines : 2 * lines, :].astype(F32) * factor
    gs_ref[2] = low.T[0:hid]
    for k in range(3):
        gt_ref[k] = low[k * half : (k + 1) * half, hid : 2 * hid]
    gb_ref[...] = low[3 * half : 3 * half + 1, hid : 2 * hid]

    pl.when(has_r)(y_right.wait_send)
    pl.when(has_l)(y_left.wait_send)
    g_left.wait_send()
    g_right.wait_send()
    m_right.wait_send()
    m_left.wait_send()

    @pl.when(has_r)
    def _():
        for t in range(frames):
            p_right(t).wait_send()

    @pl.when(has_l)
    def _():
        for t in range(frames):
            p_left(t).wait_send()

    rs0.wait_send()
    rs1.wait_send()
    for level in range(2, last):
        ex(level).wait_send()
    ag1.wait_send()
    ag0.wait_send()


def shards(gz_count, ta_count, outputs_fwd, cotangent, spatial_weight, hidden_bias, temporal_weight):
    frames, planes, channels, pix = outputs_fwd.shape
    half = channels // 2
    hid = spatial_weight.shape[1]
    window = 9 * half
    wcat = spatial_weight.transpose((1, 0, 2)).reshape((hid, 3 * window))
    flip = (
        spatial_weight.reshape((3, hid, 9, half))[:, :, ::-1]
        .transpose((0, 3, 2, 1))
        .reshape((3 * half, 9 * hid))
    )
    tw = temporal_weight.reshape((3 * half, hid))
    factor = 1.0 / math.sqrt(frames * ta_count * planes * gz_count * ROWS * COLS)
    vmem = pl.BlockSpec(memory_space=pltpu.VMEM)
    lines = window
    count = len(levels_of(gz_count, ta_count))
    dma = pltpu.SemaphoreType.DMA
    field = jax.ShapeDtypeStruct((frames, planes, half, pix), BF16)
    outs = pl.pallas_call(
        functools.partial(kernel, gz_count, ta_count, factor),
        out_shape=(
            field,
            field,
            jax.ShapeDtypeStruct((3, hid, window), F32),
            jax.ShapeDtypeStruct((1, hid), F32),
            jax.ShapeDtypeStruct((3, half, hid), F32),
        ),
        in_specs=[vmem] * 6,
        out_specs=(vmem,) * 5,
        scratch_shapes=[
            pltpu.VMEM((frames, (planes + 2) * window, pix), BF16),
            pltpu.VMEM((frames * planes, 9 * hid, pix), BF16),
            pltpu.VMEM((frames, planes, 3 * half, pix), BF16),
            pltpu.VMEM((2, frames, half, pix), BF16),
            pltpu.VMEM((frames, planes, hid, pix), F32),
            pltpu.VMEM((frames, planes, hid, pix), BF16),
            pltpu.VMEM((frames, planes, hid, pix), BF16),
            pltpu.VMEM((frames, planes, 3 * half, pix), F32),
            pltpu.VMEM((frames, planes, 3 * half, pix), F32),
            pltpu.VMEM((2, planes, half, pix), BF16),
            pltpu.VMEM((2, planes, half, pix), BF16),
            pltpu.VMEM((2, frames, half, pix), BF16),
            pltpu.VMEM((2, frames, half, pix), BF16),
            pltpu.VMEM((2 * lines, 2 * hid), F32),
            pltpu.VMEM((lines, 2 * hid), BF16),
            pltpu.VMEM((lines, 2 * hid), BF16),
            pltpu.VMEM((lines, 2 * hid), F32),
            pltpu.VMEM((lines // 2, 2 * hid), BF16),
            pltpu.VMEM((lines // 2, 2 * hid), BF16),
            pltpu.VMEM((max(count - 2, 1), lines // 2, 2 * hid), BF16),
            pltpu.VMEM((max(count - 2, 1), lines // 2, 2 * hid), BF16),
            pltpu.VMEM((2 * lines, 2 * hid), BF16),
            dma((2,)), dma((2,)), dma((2,)), dma((2,)), dma((2,)), dma((2,)),
            dma((2, frames)), dma((2, frames)), dma((count + 2,)), dma((count + 2,)),
        ],
        compiler_params=pltpu.CompilerParams(
            collective_id=0, has_side_effects=True, vmem_limit_bytes=56 * 1024 * 1024
        ),
    )(outputs_fwd, cotangent, wcat, flip, hidden_bias[:, None], tw)
    return outs[0], outs[1], outs[2], outs[3].reshape((hid,)), outs[4]


def solution(mesh):
    placed = (P("ta", "gz", None, None), P("ta", "gz", None, None), P(), P(), P())
    return jax.shard_map(
        functools.partial(shards, mesh.shape["gz"], mesh.shape["ta"]),
        mesh=mesh,
        in_specs=placed,
        out_specs=(P("ta", "gz", None, None), P("ta", "gz", None, None), P(), P(), P()),
        check_vma=False,
    )
```

time: 340 us -> 48.7 us (0.14)
  waiting for transfers between devices: 124 us -> 0 us
  local copies, waits for them, and re-layouts: 109 us -> 9.2 us
  blocking collectives: 41.7 us -> 0 us
  Pallas kernels: 0 us -> 38.5 us
  matrix products: 28.3 us -> 0 us
  starting transfers between devices: 13.8 us -> 0 us
  between operations: 14.4 us -> 0.69 us
  other arithmetic: 6.97 us -> 0 us
    psum x1 -> x0, waiting for transfers between devices: 124 us -> none  [shards(): totals = lax.psum((spatial_grad, bias_grad, temporal_grad), ('gz', 'ta'))]
    slice x15 -> x0, local copies, waits for them, and re-layouts: 60.8 us -> none  [the longest x4 25.7 us: adjoint_frame(): grad_columns[0:plane_count]]
    psum x1 -> x0, blocking collectives: 41.7 us -> none  [shards(): totals = lax.psum((spatial_grad, bias_grad, temporal_grad), ('gz', 'ta'))]
    pallas_call x0 -> x1, Pallas kernels: none -> 38.5 us  [shards(): pl.pallas_call(functools.partial(kernel, gz_count, ta_count, factor), out...]
    dot_general x21 -> x0, matrix products: 28.3 us -> none  [the longest x3 3.28 us: shards(): jnp.einsum('fzor,fzir->oi', hidden_grad, columns[:, depth:depth + plane_c...]
    reshape x5 -> x2, local copies, waits for them, and re-layouts: 20 us -> 1.69 us  [the longest x1 0.89 us: shards(): flip = spatial_weight.reshape((3, hid, 9, half))[:, :, ::-1].transpose((0...]
    ppermute x8 -> x0, starting transfers between devices: 13.7 us -> none  [the longest x4 8.3 us: with_halo(): lax.ppermute(tail, axis, [(i, (i + 1) % count) for i in range(ends)])]
    unnamed x33 -> x18, local copies, waits for them, and re-layouts: 12.3 us -> 5.63 us
  transfers between devices with their start and end apart: 9 -> 0, of which waited for: 1 -> 0; matrix products, arithmetic and copies ran while one was open for 38% -> 0% of each run, Pallas kernels for 0% -> 0%
where the time goes in v1:
time: 48.7 us; the launch traced here: 48.4 us
  Pallas kernels  38.5 us (79%)
  local copies, waits for them, and re-layouts  9.2 us (19%)
  between operations  0.69 us (1%)
    pallas_call x1, Pallas kernels, shards(): pl.pallas_call(functools.partial(kernel, gz_count, ta_count, factor), out...  38.5 us
    unnamed x18, local copies, waits for them, and re-layouts  5.63 us
    transpose x1, local copies, waits for them, and re-layouts, shards(): wcat = spatial_weight.transpose((1, 0, 2)).reshape((hid, 3 * window))  1.04 us

profile of v1, /device:TPU:0, one launch (start us, length us, event | category | flops | bytes accessed | tf_op | source)
XLA Modules:
  0.0 48.4 jit_solution(13104450860150284669)
XLA Ops:
  0.6 0.0 copy-start.4
  0.6 0.6 %copy-done.4 = f32[64]{0:T(128)S(1)} copy-done((f32[64]{0:T(128)S(1)}, f32[64]{0:T(128)}, u32[]{:S(2)}) %copy-start.4) | copy-done | bytes 280
  1.3 0.7 %copy.16.bias_ref = f32[64,1]{1,0:T(8,128)} copy(f32[64,1]{0,1:T(1,128)S(1)} %bitcast.10) | data formatting | bytes 512 | tf_op jit(solution)/shard_map/broadcast_in_dim | solution.py:416
  2.0 1.0 %copy.13 = bf16[64,3,288]{2,1,0:T(4,128)(2,1)S(1)} copy(bf16[64,3,288]{2,0,1:T(8,128)(2,1)} %bitcast.8) | data formatting | bytes 221184 | tf_op jit(solution)/shard_map/transpose | solution.py:363
  3.0 0.0 copy-start
  3.0 0.8 %reshape.25.wcat_ref = bf16[64,864]{1,0:T(8,128)(2,1)} reshape(bf16[64,3,288]{2,1,0:T(4,128)(2,1)S(1)} %copy.13) | data formatting | bytes 221184 | tf_op jit(solution)/shard_map/reshape | solution.py:363
  3.8 0.1 copy-done
  4.0 0.2 copy.14
  4.2 0.1 copy.15
  4.3 0.9 %reshape.27.flip_ref = bf16[96,576]{1,0:T(8,128)(2,1)} reshape(bf16[3,32,9,64]{3,2,1,0:T(8,128)(2,1)S(1)} %copy.15) | data formatting | bytes 221184 | tf_op jit(solution)/shard_map/reshape | solution.py:367
  5.2 38.5 %shard_map.92 = (bf16[2,2,32,1280]{3,2,1,0:T(8,128)(2,1)}, bf16[2,2,32,1280]{3,2,1,0:T(8,128)(2,1)}, f32[3,64,288]{2,1,0:T(8,128)}, f32[1,64]{1,0:T(1,128)}, f32[3,32,64]{2,1,0:T(8,128)}) custom-call(bf16[2,2,64,1280]{3,2,1,0:T(8,128)(2,1)} %x_ref.1, bf16[2,2,64,1280]{3,2,1,0:T(8,128)(2,1)} %g_ref.1, bf16[64,864]{1,0:T(8,128)(2,1)} %reshape.25.wcat_ref, ...), custom_call_target="tpu_custom_call" | custom-call | tf_op jit(solution)/shard_map/pallas_call | solution.py:376
  43.7 0.0 copy-start.1
  43.7 1.8 %copy.22 = bf16[2,2,32,1280]{3,2,1,0:T(8,128)(2,1)} copy(bf16[2,2,32,1280]{3,2,1,0:T(8,128)(2,1)} %get-tuple-element.20) | data formatting | bytes 655360
  45.4 0.0 copy-done.1
  45.4 0.0 copy-start.2
  45.4 0.7 %copy.23 = bf16[2,2,32,1280]{3,2,1,0:T(8,128)(2,1)} copy(bf16[2,2,32,1280]{3,2,1,0:T(8,128)(2,1)S(1)} %copy-done.1) | data formatting | bytes 655360
  46.2 0.4 copy-done.2
  46.5 0.0 copy-start.5
  46.5 0.0 copy-start.3
  46.5 0.7 %copy.24 = f32[3,64,288]{2,1,0:T(8,128)} copy(f32[3,64,288]{2,1,0:T(8,128)S(1)} %copy-done.2) | data formatting | bytes 442368
  47.2 0.0 copy-done.5
  47.2 0.5 %copy.25 = f32[64]{0:T(128)} copy(f32[64]{0:T(128)S(1)} %bitcast.11) | data formatting | bytes 512
  47.8 0.0 copy-done.3
  47.8 0.6 %copy.26 = f32[3,32,64]{2,1,0:T(8,128)} copy(f32[3,32,64]{2,1,0:T(8,128)S(1)} %copy-done.3) | data formatting | bytes 49152
  (1 shorter events, 0.0 us)
Async XLA Ops:
  0.6 0.7 %copy-start.4 = (f32[64]{0:T(128)S(1)}, f32[64]{0:T(128)}, u32[]{:S(2)}) copy-start(f32[64]{0:T(128)} %param.8) | copy-start | bytes 772
  3.0 0.9 %copy-start = (bf16[3,64,288]{2,1,0:T(8,128)(2,1)S(1)}, bf16[3,64,288]{2,1,0:T(8,128)(2,1)}, u32[]{:S(2)}) copy-start(bf16[3,64,288]{2,1,0:T(8,128)(2,1)} %param.7) | copy-start | bytes 331780
  43.7 1.8 %copy-start.1 = (bf16[2,2,32,1280]{3,2,1,0:T(8,128)(2,1)S(1)}, bf16[2,2,32,1280]{3,2,1,0:T(8,128)(2,1)}, u32[]{:S(2)}) copy-start(bf16[2,2,32,1280]{3,2,1,0:T(8,128)(2,1)} %get-tuple-element.21) | copy-start | bytes 983044
  45.4 1.1 %copy-start.2 = (f32[3,64,288]{2,1,0:T(8,128)S(1)}, f32[3,64,288]{2,1,0:T(8,128)}, u32[]{:S(2)}) copy-start(f32[3,64,288]{2,1,0:T(8,128)} %get-tuple-element.22) | copy-start | bytes 663556
  46.5 0.7 %copy-start.5 = (f32[1,64]{1,0:T(1,128)S(1)}, f32[1,64]{1,0:T(1,128)}, u32[]{:S(2)}) copy-start(f32[1,64]{1,0:T(1,128)} %get-tuple-element.13) | copy-start | bytes 772
  46.5 1.2 %copy-start.3 = (f32[3,32,64]{2,1,0:T(8,128)S(1)}, f32[3,32,64]{2,1,0:T(8,128)}, u32[]{:S(2)}) copy-start(f32[3,32,64]{2,1,0:T(8,128)} %get-tuple-element.24) | copy-start | bytes 73732

commit v2 on v1

v2 whole, which is shorter than its diff:
```python
import functools
import math

import jax
import jax.numpy as jnp
from jax import lax
from jax.experimental import pallas as pl
from jax.experimental.pallas import tpu as pltpu
from jax.sharding import PartitionSpec as P

ROWS = 8
COLS = 160
F32 = jnp.float32
BF16 = jnp.bfloat16


def groups_of(gz_count, ta_count):
    bits = lambda count: [1 << i for i in range(count.bit_length() - 1)]
    gz_bits = [("gz", bit) for bit in bits(gz_count)]
    ta_bits = [("ta", bit) for bit in bits(ta_count)]
    return gz_bits[:2] + ta_bits[:1], gz_bits[2:] + ta_bits[1:]


def slot_rows(window, cube):
    return -(-2 * window // (16 * cube)) * 16


def nn(lhs, rhs):
    return lax.dot_general(lhs, rhs, (((1,), (0,)), ((), ())), preferred_element_type=F32)


def nt(lhs, rhs):
    return lax.dot_general(lhs, rhs, (((1,), (1,)), ((), ())), preferred_element_type=F32)


def tn(lhs, rhs):
    return lax.dot_general(lhs, rhs, (((0,), (0,)), ((), ())), preferred_element_type=F32)


def kernel(
    gz_count, ta_count,
    x_ref, g_ref, sw_ref, bias_ref, tw_ref,
    rebuilt_ref, gin_ref, fin,
    cols, hcols, g3, yh, slope, act, hgr, parts, mown, msend, mrecv, psend, precv,
    wcat, flip, acc, accb, first, second,
    ysem_s, ysem_r, gsem_s, gsem_r, msem_s, msem_r, psem_s, psem_r,
    asem_s, asem_r, bsem_s, bsem_r, csem_s, csem_r,
):
    frames, planes = x_ref.shape[0], x_ref.shape[1]
    half = x_ref.shape[2] // 2
    pix = x_ref.shape[3]
    hid = bias_ref.shape[1]
    me_g = lax.axis_index("gz")
    me_t = lax.axis_index("ta")
    has_l = me_g > 0
    has_r = me_g < gz_count - 1
    mesh_id = pl.DeviceIdType.MESH
    ta_r = lax.rem(me_t + 1, ta_count)
    ta_l = lax.rem(me_t + ta_count - 1, ta_count)
    near_bits, far_bits = groups_of(gz_count, ta_count)

    def member(group, flip_mask):
        place = {"gz": me_g, "ta": me_t}
        index = 0
        for order, (axis, bit) in enumerate(group):
            at = me_g if axis == "gz" else me_t
            has = lax.rem(at // bit, 2)
            if flip_mask >> order & 1:
                place[axis] = place[axis] + bit - 2 * bit * has
                has = 1 - has
            index = index + (has << order)
        return (place["gz"], place["ta"]), index

    near_count, far_count = 1 << len(near_bits), 1 << len(far_bits)

    barrier = pltpu.get_barrier_semaphore()

    def greet(dev):
        pl.semaphore_signal(barrier, inc=1, device_id=dev, device_id_type=mesh_id)

    greet((me_g, ta_r))
    greet((me_g, ta_l))
    for j in range(1, near_count):
        greet(member(near_bits, j)[0])
    for j in range(1, far_count):
        greet(member(far_bits, j)[0])

    @pl.when(has_l)
    def _():
        greet((me_g - 1, me_t))

    @pl.when(has_r)
    def _():
        greet((me_g + 1, me_t))

    window = 9 * half
    for dz in range(3):
        wcat[:, dz * window : (dz + 1) * window] = sw_ref[dz]
        turned = sw_ref[dz].astype(F32).T.astype(BF16)
        for w in range(9):
            flip[dz * half : (dz + 1) * half, w * hid : (w + 1) * hid] = turned[(8 - w) * half : (9 - w) * half]
    bias = jnp.broadcast_to(bias_ref[...], (8, hid)).T[:, 0:1]
    beside = has_l.astype(jnp.int32) + has_r.astype(jnp.int32)
    pl.semaphore_wait(barrier, near_count + far_count + beside)

    def remote(src, dst, ssem, rsem, dev):
        return pltpu.make_async_remote_copy(
            src_ref=src, dst_ref=dst, send_sem=ssem, recv_sem=rsem, device_id=dev, device_id_type=mesh_id
        )

    y_right = remote(x_ref.at[:, planes - 1, 0:half], yh.at[0], ysem_s.at[0], ysem_r.at[0], (me_g + 1, me_t))
    y_left = remote(x_ref.at[:, 0, 0:half], yh.at[1], ysem_s.at[1], ysem_r.at[1], (me_g - 1, me_t))
    g_left = [
        remote(
            g_ref.at[0, z, half : 2 * half], g3.at[frames - 1, z, 0:half],
            gsem_s.at[0, z], gsem_r.at[0, z], (me_g, ta_l),
        )
        for z in range(planes)
    ]
    g_right = [
        remote(
            g_ref.at[frames - 1, z, half : 2 * half], g3.at[0, z, 2 * half : 3 * half],
            gsem_s.at[1, z], gsem_r.at[1, z], (me_g, ta_r),
        )
        for z in range(planes)
    ]
    pl.when(has_r)(y_right.start)
    pl.when(has_l)(y_left.start)
    for z in range(planes):
        g_left[z].start()
        g_right[z].start()

    for s in range(frames):
        for z in range(planes):
            for k in range(3):
                t = s + 1 - k
                if 0 <= t < frames:
                    g3[s, z, k * half : (k + 1) * half, :] = g_ref[t, z, half : 2 * half, :]

    place = lax.broadcasted_iota(jnp.int32, (1, pix), 1)
    column = lax.rem(place, COLS)
    col_ok = {-1: column > 0, 1: column < COLS - 1}
    row_ok = {-1: place >= COLS, 1: place < pix - COLS}

    def unfold(value, store):
        for c in (-1, 0, 1):
            moved = value
            if c != 0:
                moved = jnp.where(col_ok[c], pltpu.roll(value, (-c) % pix, 1), 0.0)
            for r in (-1, 0, 1):
                out = moved
                if r != 0:
                    out = jnp.where(row_ok[r], pltpu.roll(moved, (-r * COLS) % pix, 1), 0.0)
                store(3 * (r + 1) + c + 1, out.astype(BF16))

    def unfold_y(value, t, plane):
        def store(w, out):
            base = plane * window + w * half
            cols[t, base : base + half, :] = out

        unfold(value.astype(F32), store)

    for t in range(frames):
        for z in range(planes):
            unfold_y(x_ref[t, z, 0:half, :], t, z + 1)

    @pl.when(has_l)
    def _():
        y_right.wait_recv()
        for t in range(frames):
            unfold_y(yh[0, t], t, 0)

    @pl.when(jnp.logical_not(has_l))
    def _():
        for t in range(frames):
            cols[t, 0:window, :] = jnp.zeros((window, pix), BF16)

    @pl.when(has_r)
    def _():
        y_left.wait_recv()
        for t in range(frames):
            unfold_y(yh[1, t], t, planes + 1)

    @pl.when(jnp.logical_not(has_r))
    def _():
        for t in range(frames):
            cols[t, (planes + 1) * window : (planes + 2) * window, :] = jnp.zeros((window, pix), BF16)

    whole = wcat[...]
    tw = tw_ref[...]
    for t in range(frames):
        for z in range(planes):
            pre = nn(whole, cols[t, z * window : (z + 3) * window, :]) + bias
            sig = jax.nn.sigmoid(pre)
            active = (pre * sig).astype(BF16)
            slope[t, z] = sig * (1.0 + pre * (1.0 - sig))
            act[t, z] = active
            mown[t, z] = nn(tw, active)
        if t == 0:
            for z in range(planes):
                msend[1, z] = mown[0, z, 2 * half : 3 * half, :].astype(BF16)
        if t == frames - 1:
            for z in range(planes):
                msend[0, z] = mown[t, z, 0:half, :].astype(BF16)
    m_right = remote(msend.at[0], mrecv.at[0], msem_s.at[0], msem_r.at[0], (me_g, ta_r))
    m_left = remote(msend.at[1], mrecv.at[1], msem_s.at[1], msem_r.at[1], (me_g, ta_l))
    m_right.start()

    ones = jnp.ones((8, pix), BF16)
    ssum = jnp.zeros((3 * window, hid), F32)
    tsum = jnp.zeros((3 * half, hid), F32)
    bsum = jnp.zeros((8, hid), F32)
    for z in range(planes):
        g_left[z].wait_recv()
        g_right[z].wait_recv()
        for t in range(frames):
            around = g3[t, z]
            hgrad = (tn(tw, around) * slope[t, z]).astype(BF16)
            hgr[t, z] = hgrad
            tsum = tsum + nt(around, act[t, z])
            bsum = bsum + nt(ones, hgrad)
            ssum = ssum + nt(cols[t, z * window : (z + 3) * window, :], hgrad)
    acc[0:window, 0:hid] = ssum[0:window]
    acc[0:window, hid : 2 * hid] = ssum[window : 2 * window]
    acc[window : 2 * window, 0:hid] = ssum[2 * window : 3 * window]
    used = window + 3 * half
    acc[window:used, hid : 2 * hid] = tsum
    acc[used : used + 8, hid : 2 * hid] = bsum
    acc[used + 8 : 2 * window, hid : 2 * hid] = jnp.zeros((2 * window - used - 8, hid), F32)
    if acc.shape[0] > 2 * window:
        acc[2 * window :, :] = jnp.zeros((acc.shape[0] - 2 * window, 2 * hid), F32)
    accb[...] = acc[...].astype(BF16)

    rows = acc.shape[0] // near_count

    def span(index):
        return pl.ds(pl.multiple_of(index * rows, 16), rows)

    near_me = member(near_bits, 0)[1]
    far_me = member(far_bits, 0)[1]
    scatter, share, gather = [], [], []
    for j in range(1, near_count):
        dev, index = member(near_bits, j)
        scatter.append(remote(accb.at[span(index)], first.at[j - 1], asem_s.at[j - 1], asem_r.at[j - 1], dev))
        mine = fin.at[span(near_me)]
        gather.append(remote(mine, mine, csem_s.at[j - 1], csem_r.at[j - 1], dev))
    for j in range(1, far_count):
        dev, _ = member(far_bits, j)
        share.append(remote(second.at[far_me], second.at[far_me], bsem_s.at[j - 1], bsem_r.at[j - 1], dev))
    for copy in scatter:
        copy.start()
    m_left.start()

    def step_share():
        total = acc[span(near_me), :]
        for j, copy in enumerate(scatter):
            copy.wait_recv()
            total = total + first[j].astype(F32)
        second[pl.ds(far_me, 1)] = total.astype(BF16)[None]
        for copy in share:
            copy.start()

    def step_gather():
        for copy in share:
            copy.wait_recv()
        total = second[0].astype(F32)
        for j in range(1, far_count):
            total = total + second[j].astype(F32)
        fin[span(near_me), :] = total.astype(BF16)
        for copy in gather:
            copy.start()

    back = flip[...]

    def p_right(t):
        return remote(psend.at[0, t], precv.at[0, t], psem_s.at[0, t], psem_r.at[0, t], (me_g + 1, me_t))

    def p_left(t):
        return remote(psend.at[1, t], precv.at[1, t], psem_s.at[1, t], psem_r.at[1, t], (me_g - 1, me_t))

    for t in range(frames):
        for z in range(planes):
            at = t * planes + z

            def store(w, out):
                hcols[at, w * hid : (w + 1) * hid, :] = out

            unfold(hgr[t, z].astype(F32), store)
            parts[t, z] = nn(back, hcols[at])
            if z == 0:
                psend[1, t] = parts[t, z, 0:half, :].astype(BF16)
                pl.when(has_l)(p_left(t).start)
            if z == planes - 1:
                psend[0, t] = parts[t, z, 2 * half : 3 * half, :].astype(BF16)
                pl.when(has_r)(p_right(t).start)
            if at == max(frames * planes - 2, 0):
                step_share()

    m_right.wait_recv()
    m_left.wait_recv()
    for t in range(frames):
        for z in range(planes):
            total = mown[t, z, half : 2 * half, :]
            total = total + (mown[t - 1, z, 0:half, :] if t > 0 else mrecv[0, z].astype(F32))
            total = total + (mown[t + 1, z, 2 * half : 3 * half, :] if t < frames - 1 else mrecv[1, z].astype(F32))
            rebuilt_ref[t, z] = (x_ref[t, z, half : 2 * half, :].astype(F32) - total).astype(BF16)
    step_gather()

    @pl.when(has_l)
    def _():
        for t in range(frames):
            p_right(t).wait_recv()

    @pl.when(jnp.logical_not(has_l))
    def _():
        precv[0] = jnp.zeros_like(precv[0])

    @pl.when(has_r)
    def _():
        for t in range(frames):
            p_left(t).wait_recv()

    @pl.when(jnp.logical_not(has_r))
    def _():
        precv[1] = jnp.zeros_like(precv[1])

    for t in range(frames):
        for z in range(planes):
            total = parts[t, z, half : 2 * half, :]
            total = total + (parts[t, z - 1, 2 * half : 3 * half, :] if z > 0 else precv[0, t].astype(F32))
            total = total + (parts[t, z + 1, 0:half, :] if z < planes - 1 else precv[1, t].astype(F32))
            gin_ref[t, z] = (g_ref[t, z, 0:half, :].astype(F32) + total).astype(BF16)

    for copy in gather:
        copy.wait_recv()

    pl.when(has_r)(y_right.wait_send)
    pl.when(has_l)(y_left.wait_send)
    for z in range(planes):
        g_left[z].wait_send()
        g_right[z].wait_send()
    m_right.wait_send()
    m_left.wait_send()

    @pl.when(has_r)
    def _():
        for t in range(frames):
            p_right(t).wait_send()

    @pl.when(has_l)
    def _():
        for t in range(frames):
            p_left(t).wait_send()

    for copy in scatter + share + gather:
        copy.wait_send()


def finish(factor, rebuilt_in, gin_in, fin, rebuilt_ref, gin_ref, gs_ref, gb_ref, gt_ref):
    hid, window = gs_ref.shape[1], gs_ref.shape[2]
    half = window // 9
    rebuilt_ref[...] = rebuilt_in[...]
    gin_ref[...] = gin_in[...]
    turned = (fin[0:window, :].astype(F32) * factor).T
    gs_ref[0] = turned[0:hid]
    gs_ref[1] = turned[hid : 2 * hid]
    low = fin[window : 2 * window, :].astype(F32) * factor
    gs_ref[2] = low.T[0:hid]
    for k in range(3):
        gt_ref[k] = low[k * half : (k + 1) * half, hid : 2 * hid]
    gb_ref[...] = low[3 * half : 3 * half + 1, hid : 2 * hid]


def shards(gz_count, ta_count, outputs_fwd, cotangent, spatial_weight, hidden_bias, temporal_weight):
    frames, planes, channels, pix = outputs_fwd.shape
    half = channels // 2
    hid = spatial_weight.shape[1]
    window = 9 * half
    tw = temporal_weight.reshape((3 * half, hid))
    factor = 1.0 / math.sqrt(frames * ta_count * planes * gz_count * ROWS * COLS)
    vmem = pl.BlockSpec(memory_space=pltpu.VMEM)
    near_bits, far_bits = groups_of(gz_count, ta_count)
    near_count, far_count = 1 << len(near_bits), 1 << len(far_bits)
    rows = slot_rows(window, near_count)
    dma = pltpu.SemaphoreType.DMA
    field = jax.ShapeDtypeStruct((frames, planes, half, pix), BF16)
    outs = pl.pallas_call(
        functools.partial(kernel, gz_count, ta_count),
        out_shape=(
            field,
            field,
            jax.ShapeDtypeStruct((near_count * rows, 2 * hid), BF16),
        ),
        in_specs=[vmem] * 5,
        out_specs=(vmem,) * 3,
        scratch_shapes=[
            pltpu.VMEM((frames, (planes + 2) * window, pix), BF16),
            pltpu.VMEM((frames * planes, 9 * hid, pix), BF16),
            pltpu.VMEM((frames, planes, 3 * half, pix), BF16),
            pltpu.VMEM((2, frames, half, pix), BF16),
            pltpu.VMEM((frames, planes, hid, pix), F32),
            pltpu.VMEM((frames, planes, hid, pix), BF16),
            pltpu.VMEM((frames, planes, hid, pix), BF16),
            pltpu.VMEM((frames, planes, 3 * half, pix), F32),
            pltpu.VMEM((frames, planes, 3 * half, pix), F32),
            pltpu.VMEM((2, planes, half, pix), BF16),
            pltpu.VMEM((2, planes, half, pix), BF16),
            pltpu.VMEM((2, frames, half, pix), BF16),
            pltpu.VMEM((2, frames, half, pix), BF16),
            pltpu.VMEM((hid, 3 * window), BF16),
            pltpu.VMEM((3 * half, 9 * hid), BF16),
            pltpu.VMEM((near_count * rows, 2 * hid), F32),
            pltpu.VMEM((near_count * rows, 2 * hid), BF16),
            pltpu.VMEM((near_count - 1, rows, 2 * hid), BF16),
            pltpu.VMEM((far_count, rows, 2 * hid), BF16),
            dma((2,)), dma((2,)), dma((2, planes)), dma((2, planes)), dma((2,)), dma((2,)),
            dma((2, frames)), dma((2, frames)),
            dma((near_count - 1,)), dma((near_count - 1,)),
            dma((far_count - 1,)), dma((far_count - 1,)),
            dma((near_count - 1,)), dma((near_count - 1,)),
        ],
        compiler_params=pltpu.CompilerParams(
            collective_id=0, has_side_effects=True, vmem_limit_bytes=36 * 1024 * 1024
        ),
    )(outputs_fwd, cotangent, spatial_weight, hidden_bias[None, :], tw)
    ends = pl.pallas_call(
        functools.partial(finish, factor),
        out_shape=(
            field,
            field,
            jax.ShapeDtypeStruct((3, hid, window), F32),
            jax.ShapeDtypeStruct((1, hid), F32),
            jax.ShapeDtypeStruct((3, half, hid), F32),
        ),
        in_specs=[vmem] * 3,
        out_specs=(vmem,) * 5,
        compiler_params=pltpu.CompilerParams(vmem_limit_bytes=8 * 1024 * 1024),
    )(*outs)
    return ends[0], ends[1], ends[2], ends[3].reshape((hid,)), ends[4]


def solution(mesh):
    placed = (P("ta", "gz", None, None), P("ta", "gz", None, None), P(), P(), P())
    return jax.shard_map(
        functools.partial(shards, mesh.shape["gz"], mesh.shape["ta"]),
        mesh=mesh,
        in_specs=placed,
        out_specs=(P("ta", "gz", None, None), P("ta", "gz", None, None), P(), P(), P()),
        check_vma=False,
    )
```

time: 48.7 us -> 37.2 us (0.76)
  Pallas kernels: 38.5 us -> 31.8 us
  local copies, waits for them, and re-layouts: 9.2 us -> 4.47 us
    pallas_call x1 -> x2, Pallas kernels: 38.5 us -> 31.8 us  [the longest x1 30.7 us: shards(): pl.pallas_call(functools.partial(kernel, gz_count, ta_count), out_shape=(...]
    reshape x2 -> x0, local copies, waits for them, and re-layouts: 1.69 us -> none  [the longest x1 0.89 us: shards(): flip = spatial_weight.reshape((3, hid, 9, half))[:, :, ::-1].transpose((0...]
    transpose x3 -> x0, local copies, waits for them, and re-layouts: 1.17 us -> none  [the longest x1 1.04 us: shards(): wcat = spatial_weight.transpose((1, 0, 2)).reshape((hid, 3 * window))]
    unnamed x18 -> x10, local copies, waits for them, and re-layouts: 5.63 us -> 4.47 us
    broadcast_in_dim x1 -> x0, local copies, waits for them, and re-layouts: 0.71 us -> none  [shards(): hidden_bias[:, None]]
where the time goes in v2:
time: 37.2 us; the launch traced here: 36.9 us
  Pallas kernels  31.8 us (85%)
  local copies, waits for them, and re-layouts  4.47 us (12%)
  between operations  0.65 us (2%)
    pallas_call x1, Pallas kernels, shards(): pl.pallas_call(functools.partial(kernel, gz_count, ta_count), out_shape=(...  30.7 us
    unnamed x10, local copies, waits for them, and re-layouts  4.47 us
    pallas_call x1, Pallas kernels, shards(): pl.pallas_call(functools.partial(finish, factor), out_shape=(field, field...  1.08 us

profile of v2, /device:TPU:0, one launch (start us, length us, event | category | flops | bytes accessed | tf_op | source)
XLA Modules:
  0.0 36.9 jit_solution(12459642409480584145)
XLA Ops:
  0.6 0.0 copy-start.4
  0.6 0.6 %copy-done.4 = f32[64]{0:T(128)S(1)} copy-done((f32[64]{0:T(128)S(1)}, f32[64]{0:T(128)}, u32[]{:S(2)}) %copy-start.4) | copy-done | bytes 280
  1.3 0.0 copy-start
  1.3 1.1 %copy-done = bf16[2,2,64,1280]{3,2,1,0:T(8,128)(2,1)S(1)} copy-done((bf16[2,2,64,1280]{3,2,1,0:T(8,128)(2,1)S(1)}, bf16[2,2,64,1280]{3,2,1,0:T(8,128)(2,1)}, u32[]{:S(2)}) %copy-start) | copy-done | bytes 655384
  2.4 0.0 copy-start.1
  2.4 1.1 %copy-done.1 = bf16[2,2,64,1280]{3,2,1,0:T(8,128)(2,1)S(1)} copy-done((bf16[2,2,64,1280]{3,2,1,0:T(8,128)(2,1)S(1)}, bf16[2,2,64,1280]{3,2,1,0:T(8,128)(2,1)}, u32[]{:S(2)}) %copy-start.1) | copy-done | bytes 655384
  3.5 0.0 copy-start.2
  3.5 0.9 %copy-done.2 = bf16[3,64,288]{2,1,0:T(8,128)(2,1)S(1)} copy-done((bf16[3,64,288]{2,1,0:T(8,128)(2,1)S(1)}, bf16[3,64,288]{2,1,0:T(8,128)(2,1)}, u32[]{:S(2)}) %copy-start.2) | copy-done | bytes 110616
  4.4 0.0 copy-start.3
  4.4 0.7 %copy-done.3 = bf16[3,32,64]{2,1,0:T(8,128)(2,1)S(1)} copy-done((bf16[3,32,64]{2,1,0:T(8,128)(2,1)S(1)}, bf16[3,32,64]{2,1,0:T(8,128)(2,1)}, u32[]{:S(2)}) %copy-start.3) | copy-done | bytes 12312
  5.1 30.7 %shard_map.92 = (bf16[2,2,32,1280]{3,2,1,0:T(8,128)(2,1)S(1)}, bf16[2,2,32,1280]{3,2,1,0:T(8,128)(2,1)S(1)}, bf16[640,128]{1,0:T(8,128)(2,1)S(1)}) custom-call(bf16[2,2,64,1280]{3,2,1,0:T(8,128)(2,1)S(1)} %copy-done, bf16[2,2,64,1280]{3,2,1,0:T(8,128)(2,1)S(1)} %copy-done.1, bf16[3,64,288]{2,1,0:T(8,128)(2,1)S(1)} %copy-done.2, f32[1,64]{1,0:T(1,128)S(1)} %bitcast.4, ...), custom_call_target="tpu_custom_call" | custom-call | tf_op jit(solution)/shard_map/pallas_call | solution.py:387
  35.8 1.1 %shard_map.93 = (bf16[2,2,32,1280]{3,2,1,0:T(8,128)(2,1)}, bf16[2,2,32,1280]{3,2,1,0:T(8,128)(2,1)}, f32[3,64,288]{2,1,0:T(8,128)}, f32[1,64]{1,0:T(1,128)}, f32[3,32,64]{2,1,0:T(8,128)}) custom-call(bf16[2,2,32,1280]{3,2,1,0:T(8,128)(2,1)S(1)} %get-tuple-element.13.rebuilt_in, bf16[2,2,32,1280]{3,2,1,0:T(8,128)(2,1)S(1)} %get-tuple-element.14.gin_in, ...), custom_call_target="tpu_custom_call" | custom-call | tf_op jit(solution)/shard_map/pallas_call | solution.py:426
Async XLA Ops:
  0.6 0.7 %copy-start.4 = (f32[64]{0:T(128)S(1)}, f32[64]{0:T(128)}, u32[]{:S(2)}) copy-start(f32[64]{0:T(128)} %param.8) | copy-start | bytes 772
  1.3 1.1 %copy-start = (bf16[2,2,64,1280]{3,2,1,0:T(8,128)(2,1)S(1)}, bf16[2,2,64,1280]{3,2,1,0:T(8,128)(2,1)}, u32[]{:S(2)}) copy-start(bf16[2,2,64,1280]{3,2,1,0:T(8,128)(2,1)} %x_ref.1) | copy-start | bytes 1966084
  2.4 1.1 %copy-start.1 = (bf16[2,2,64,1280]{3,2,1,0:T(8,128)(2,1)S(1)}, bf16[2,2,64,1280]{3,2,1,0:T(8,128)(2,1)}, u32[]{:S(2)}) copy-start(bf16[2,2,64,1280]{3,2,1,0:T(8,128)(2,1)} %g_ref.1) | copy-start | bytes 1966084
  3.5 0.9 %copy-start.2 = (bf16[3,64,288]{2,1,0:T(8,128)(2,1)S(1)}, bf16[3,64,288]{2,1,0:T(8,128)(2,1)}, u32[]{:S(2)}) copy-start(bf16[3,64,288]{2,1,0:T(8,128)(2,1)} %sw_ref.1) | copy-start | bytes 331780
  4.4 0.7 %copy-start.3 = (bf16[3,32,64]{2,1,0:T(8,128)(2,1)S(1)}, bf16[3,32,64]{2,1,0:T(8,128)(2,1)}, u32[]{:S(2)}) copy-start(bf16[3,32,64]{2,1,0:T(8,128)(2,1)} %param.9) | copy-start | bytes 36868

commit v3 on v2

--- a/solution.py
+++ b/solution.py
@@ -39,10 +39,10 @@
 
 def kernel(
     gz_count, ta_count,
-    x_ref, g_ref, sw_ref, bias_ref, tw_ref,
+    x_hbm, g_hbm, sw_hbm, bias_hbm, tw_hbm,
     rebuilt_ref, gin_ref, fin,
     cols, hcols, g3, yh, slope, act, hgr, parts, mown, msend, mrecv, psend, precv,
-    wcat, flip, acc, accb, first, second,
+    x_ref, g_ref, sw_ref, bias_ref, tw_ref, lsem, wcat, flip, acc, accb, first, second,
     ysem_s, ysem_r, gsem_s, gsem_r, msem_s, msem_r, psem_s, psem_r,
     asem_s, asem_r, bsem_s, bsem_r, csem_s, csem_r,
 ):
@@ -73,6 +73,8 @@
 
     near_count, far_count = 1 << len(near_bits), 1 << len(far_bits)
 
+    pairs = ((sw_hbm, sw_ref), (bias_hbm, bias_ref), (tw_hbm, tw_ref), (x_hbm, x_ref), (g_hbm, g_ref))
+    loads = [pltpu.make_async_copy(src, dst, lsem.at[i]) for i, (src, dst) in enumerate(pairs)]
     barrier = pltpu.get_barrier_semaphore()
 
     def greet(dev):
@@ -93,6 +95,10 @@
     def _():
         greet((me_g + 1, me_t))
 
+    for load in loads:
+        load.start()
+    for load in loads[:3]:
+        load.wait()
     window = 9 * half
     for dz in range(3):
         wcat[:, dz * window : (dz + 1) * window] = sw_ref[dz]
@@ -108,18 +114,18 @@
             src_ref=src, dst_ref=dst, send_sem=ssem, recv_sem=rsem, device_id=dev, device_id_type=mesh_id
         )
 
-    y_right = remote(x_ref.at[:, planes - 1, 0:half], yh.at[0], ysem_s.at[0], ysem_r.at[0], (me_g + 1, me_t))
-    y_left = remote(x_ref.at[:, 0, 0:half], yh.at[1], ysem_s.at[1], ysem_r.at[1], (me_g - 1, me_t))
+    y_right = remote(x_hbm.at[:, planes - 1, 0:half], yh.at[0], ysem_s.at[0], ysem_r.at[0], (me_g + 1, me_t))
+    y_left = remote(x_hbm.at[:, 0, 0:half], yh.at[1], ysem_s.at[1], ysem_r.at[1], (me_g - 1, me_t))
     g_left = [
         remote(
-            g_ref.at[0, z, half : 2 * half], g3.at[frames - 1, z, 0:half],
+            g_hbm.at[0, z, half : 2 * half], g3.at[frames - 1, z, 0:half],
             gsem_s.at[0, z], gsem_r.at[0, z], (me_g, ta_l),
         )
         for z in range(planes)
     ]
     g_right = [
         remote(
-            g_ref.at[frames - 1, z, half : 2 * half], g3.at[0, z, 2 * half : 3 * half],
+            g_hbm.at[frames - 1, z, half : 2 * half], g3.at[0, z, 2 * half : 3 * half],
             gsem_s.at[1, z], gsem_r.at[1, z], (me_g, ta_r),
         )
         for z in range(planes)
@@ -130,6 +136,8 @@
         g_left[z].start()
         g_right[z].start()
 
+    for load in loads[3:]:
+        load.wait()
     for s in range(frames):
         for z in range(planes):
             for k in range(3):
@@ -391,7 +399,7 @@
             field,
             jax.ShapeDtypeStruct((near_count * rows, 2 * hid), BF16),
         ),
-        in_specs=[vmem] * 5,
+        in_specs=[pl.BlockSpec(memory_space=pltpu.HBM)] * 5,
         out_specs=(vmem,) * 3,
         scratch_shapes=[
             pltpu.VMEM((frames, (planes + 2) * window, pix), BF16),
@@ -407,6 +415,12 @@
             pltpu.VMEM((2, planes, half, pix), BF16),
             pltpu.VMEM((2, frames, half, pix), BF16),
             pltpu.VMEM((2, frames, half, pix), BF16),
+            pltpu.VMEM(outputs_fwd.shape, BF16),
+            pltpu.VMEM(cotangent.shape, BF16),
+            pltpu.VMEM(spatial_weight.shape, BF16),
+            pltpu.VMEM((1, hid), F32),
+            pltpu.VMEM(tw.shape, BF16),
+            dma((5,)),
             pltpu.VMEM((hid, 3 * window), BF16),
             pltpu.VMEM((3 * half, 9 * hid), BF16),
             pltpu.VMEM((near_count * rows, 2 * hid), F32),
@@ -420,7 +434,7 @@
             dma((near_count - 1,)), dma((near_count - 1,)),
         ],
         compiler_params=pltpu.CompilerParams(
-            collective_id=0, has_side_effects=True, vmem_limit_bytes=36 * 1024 * 1024
+            collective_id=0, has_side_effects=True, vmem_limit_bytes=60 * 1024 * 1024
         ),
     )(outputs_fwd, cotangent, spatial_weight, hidden_bias[None, :], tw)
     ends = pl.pallas_call(
@@ -434,7 +448,7 @@
         ),
         in_specs=[vmem] * 3,
         out_specs=(vmem,) * 5,
-        compiler_params=pltpu.CompilerParams(vmem_limit_bytes=8 * 1024 * 1024),
+        compiler_params=pltpu.CompilerParams(vmem_limit_bytes=60 * 1024 * 1024),
     )(*outs)
     return ends[0], ends[1], ends[2], ends[3].reshape((hid,)), ends[4]
 

time: 37.2 us -> 35 us (0.941)
  local copies, waits for them, and re-layouts: 4.47 us -> 0 us
  Pallas kernels: 31.8 us -> 34.2 us
    unnamed x10 -> x0, local copies, waits for them, and re-layouts: 4.47 us -> none
    pallas_call x1, Pallas kernels: 30.7 us -> 32 us  [shards(): pl.pallas_call(functools.partial(kernel, gz_count, ta_count), out_shape=(...]
    pallas_call x1, Pallas kernels: 1.08 us -> 2.2 us  [shards(): pl.pallas_call(functools.partial(finish, factor), out_shape=(field, field...]
where the time goes in v3:
time: 35 us; the launch traced here: 34.8 us
  Pallas kernels  34.2 us (98%)
  between operations  0.64 us (2%)
    pallas_call x1, Pallas kernels, shards(): pl.pallas_call(functools.partial(kernel, gz_count, ta_count), out_shape=(...  32 us
    pallas_call x1, Pallas kernels, shards(): pl.pallas_call(functools.partial(finish, factor), out_shape=(field, field...  2.2 us

profile of v3, /device:TPU:0, one launch (start us, length us, event | category | flops | bytes accessed | tf_op | source)
XLA Modules:
  0.0 34.8 jit_solution(16099340661376004022)
XLA Ops:
  0.6 32.0 %shard_map.92 = (bf16[2,2,32,1280]{3,2,1,0:T(8,128)(2,1)}, bf16[2,2,32,1280]{3,2,1,0:T(8,128)(2,1)}, bf16[640,128]{1,0:T(8,128)(2,1)}) custom-call(bf16[2,2,64,1280]{3,2,1,0:T(8,128)(2,1)} %x_hbm.1, bf16[2,2,64,1280]{3,2,1,0:T(8,128)(2,1)} %g_hbm.1, bf16[3,64,288]{2,1,0:T(8,128)(2,1)} %sw_hbm.1, f32[1,64]{1,0:T(1,128)} %bitcast.4, bf16[96,64]{1,0:T(8,128)(2,1)} %bitcast.3), custom_call_target="tpu_custom_call" | custom-call | tf_op jit(solution)/shard_map/pallas_call | solution.py:395
  32.6 2.2 %shard_map.93 = (bf16[2,2,32,1280]{3,2,1,0:T(8,128)(2,1)}, bf16[2,2,32,1280]{3,2,1,0:T(8,128)(2,1)}, f32[3,64,288]{2,1,0:T(8,128)}, f32[1,64]{1,0:T(1,128)}, f32[3,32,64]{2,1,0:T(8,128)}) custom-call(bf16[2,2,32,1280]{3,2,1,0:T(8,128)(2,1)} %get-tuple-element.13.rebuilt_in, bf16[2,2,32,1280]{3,2,1,0:T(8,128)(2,1)} %get-tuple-element.14.gin_in, ...), custom_call_target="tpu_custom_call" | custom-call | tf_op jit(solution)/shard_map/pallas_call | solution.py:440
